TPU v7x, 128 devices: a whole 4x4x4 slice. The times are simulated.
128 devices in a mesh: energy: 32 (over y, z_lo, x), mom: 4 (over z_hi, core).
Axes of the slice: x: 4, y: 4, z: 4 (z_hi: 2, z_lo: 2; z = z_hi * 2 + z_lo), core: 2. Of those that a mesh axis runs over, the one named last changes fastest.
Arguments:
- green_ret: float32 [4, 32, 2, 10, 128, 128], P('mom', 'energy'), may hold values from -0.3125 to 0.3125
- scatter_in: float32 [4, 32, 2, 10, 128, 128], P('mom', 'energy'), may hold values from -6 to 6
- screened: float32 [4, 32, 2, 163840], P(None, None, None, ('energy', 'mom')), may hold values from -6 to 6
- momentum_table: int32 [4, 4], replicated, may hold values from 0 to 3, each once within a row
- tile_list: int32 [10, 2], replicated, may hold values from 0 to 3, as said below
Outputs:
- sigma_lesser: float32 [4, 32, 2, 10, 128, 128], P('mom', 'energy')
Inputs may be any that keep to these rules, and one draw needn't show every extreme that they name: `tile_list`: each of the 10 blocks (r, c) with |r - c| <= 1 of the 4 x 4 block grid appears in exactly one row; column 0 is the block row, column 1 the block column. `momentum_table`: each row holds every momentum index once.
All inputs are finite; a program needn't handle non-finite values.
Results may differ from a plain program's by a relative error of at most 0.0003.
Values sent between devices are 32-bit elements; how exact they have to be, the bound alone decides.
A program may use at most 384 MiB of HBM per device.

v0:
```python
import math

import jax
import jax.numpy as jnp
from jax import lax
from jax.sharding import PartitionSpec as P


def canon_positions(tile_list, nblock):
    block_rows = tile_list[:, 0]
    block_cols = tile_list[:, 1]
    offsets = block_cols - block_rows
    canon_order = jnp.where(
        offsets == 0,
        block_rows,
        jnp.where(offsets == 1, nblock + block_rows, 2 * nblock - 1 + block_cols),
    )
    tile_count = tile_list.shape[0]
    positions = jnp.arange(tile_count, dtype=jnp.int32)
    matches = (canon_order[None, :] == positions[:, None]).astype(jnp.int32)
    canon_slot = jnp.sum(matches * positions[None, :], axis=1)
    return (canon_order, canon_slot)


def canon_index(i, j, nblock):
    if i == j:
        return i
    if j == i + 1:
        return nblock + i
    return 2 * nblock - 1 + j


def neighbours(i, nblock):
    return [m for m in (i - 1, i, i + 1) if 0 <= m < nblock]


def complex_mul(left, right, adjoint):
    form = "eij,ekj->eik" if adjoint else "eij,ejk->eik"
    rr = jnp.einsum(form, left[0], right[0], precision=lax.Precision.HIGHEST)
    ii = jnp.einsum(form, left[1], right[1], precision=lax.Precision.HIGHEST)
    ri = jnp.einsum(form, left[0], right[1], precision=lax.Precision.HIGHEST)
    ir = jnp.einsum(form, left[1], right[0], precision=lax.Precision.HIGHEST)
    if adjoint:
        return (rr + ii, ir - ri)
    return (rr - ii, ri + ir)


def born_tiles(green, scatter, nblock):

    def tile_of(source, i, j):
        index = canon_index(i, j, nblock)
        return (source[:, 0, index], source[:, 1, index])

    crossed = {}
    for i in range(nblock):
        for k in neighbours(i, nblock):
            left = tile_of(green, i, k)
            for m in neighbours(k, nblock):
                product_term = complex_mul(left, tile_of(scatter, k, m), False)
                if (i, m) in crossed:
                    before = crossed[i, m]
                    crossed[i, m] = (before[0] + product_term[0], before[1] + product_term[1])
                else:
                    crossed[i, m] = product_term
    coords = (
        [(i, i) for i in range(nblock)]
        + [(i, i + 1) for i in range(nblock - 1)]
        + [(i + 1, i) for i in range(nblock - 1)]
    )
    real_tiles = []
    imag_tiles = []
    for i, j in coords:
        total_re = None
        total_im = None
        for m in neighbours(j, nblock):
            product_term = complex_mul(crossed[i, m], tile_of(green, j, m), True)
            if total_re is None:
                total_re, total_im = product_term
            else:
                total_re = total_re + product_term[0]
                total_im = total_im + product_term[1]
        real_tiles.append(total_re)
        imag_tiles.append(total_im)
    return jnp.stack([jnp.stack(real_tiles, axis=1), jnp.stack(imag_tiles, axis=1)], axis=1)


def energy_mix(pairs, screened, momentum_table):
    momenta = pairs.shape[0]
    energies = pairs.shape[1]
    pair_width = pairs.shape[3]
    padded_len = 2 * energies
    freqs = jnp.arange(padded_len, dtype=jnp.int32)
    energy_steps = jnp.arange(energies, dtype=jnp.int32)
    phases = (freqs[:, None] * energy_steps[None, :] % padded_len).astype(jnp.float32) * (
        2.0 * math.pi / padded_len
    )
    cos_table = jnp.cos(phases)
    sin_table = jnp.sin(phases)
    forward_table = jnp.concatenate([cos_table, sin_table], axis=0)
    both = jnp.concatenate([pairs, screened], axis=0).transpose((1, 0, 2, 3))
    both = both.reshape((energies, 2 * momenta * 2 * pair_width))
    spectra = jnp.dot(forward_table, both, precision=lax.Precision.HIGHEST)
    spectra = spectra.reshape((2, padded_len, 2 * momenta, 2, pair_width))
    with_cos = spectra[0]
    with_sin = spectra[1]
    spec_re = with_cos[:, :, 0] + with_sin[:, :, 1]
    spec_im = with_cos[:, :, 1] - with_sin[:, :, 0]
    green_re = spec_re[:, :momenta]
    green_im = spec_im[:, :momenta]
    screen_re = spec_re[:, momenta:]
    screen_im = spec_im[:, momenta:]
    sums_re = []
    sums_im = []
    for k in range(momenta):
        picked_re = jnp.take(green_re, momentum_table[k], axis=1)
        picked_im = jnp.take(green_im, momentum_table[k], axis=1)
        sums_re.append(jnp.sum(picked_re * screen_re - picked_im * screen_im, axis=1))
        sums_im.append(jnp.sum(picked_re * screen_im + picked_im * screen_re, axis=1))
    total_re = jnp.stack(sums_re, axis=1)
    total_im = jnp.stack(sums_im, axis=1)
    stacked = jnp.concatenate([total_re, total_im], axis=0).reshape(
        (2 * padded_len, momenta * pair_width)
    )
    cos_back = cos_table.T
    sin_back = sin_table.T
    inverse_table = jnp.concatenate(
        [
            jnp.concatenate([cos_back, -sin_back], axis=1),
            jnp.concatenate([sin_back, cos_back], axis=1),
        ],
        axis=0,
    )
    back = jnp.dot(inverse_table, stacked, precision=lax.Precision.HIGHEST) / padded_len
    back = back.reshape((2, energies, momenta, pair_width))
    scale = 1.0 / math.sqrt(momenta * energies)
    result = jnp.stack([-scale * back[1], scale * back[0]], axis=2)
    return result.transpose((1, 0, 2, 3))


def on_device(green_ret, scatter_in, screened, momentum_table, tile_list):
    k_dev = green_ret.shape[0]
    e_dev = green_ret.shape[1]
    tile_count = green_ret.shape[3]
    tile_side = green_ret.shape[4]
    nblock = (tile_count + 2) // 3
    canon_order, canon_slot = canon_positions(tile_list, nblock)
    batch_size = k_dev * e_dev
    green_canon = jnp.take(
        green_ret.reshape((batch_size, 2, tile_count, tile_side, tile_side)), canon_slot, axis=2
    )
    scatter_canon = jnp.take(
        scatter_in.reshape((batch_size, 2, tile_count, tile_side, tile_side)), canon_slot, axis=2
    )
    tiles_canon = born_tiles(green_canon, scatter_canon, nblock)
    lesser = jnp.take(tiles_canon, canon_order, axis=2).reshape(
        (k_dev, e_dev, 2, tile_count * tile_side * tile_side)
    )
    arrived = lax.all_to_all(
        lax.all_to_all(lesser, "energy", split_axis=3, concat_axis=1, tiled=True),
        "mom",
        split_axis=3,
        concat_axis=0,
        tiled=True,
    )
    mixed_pairs = energy_mix(arrived, screened, momentum_table)
    result = lax.all_to_all(
        lax.all_to_all(mixed_pairs, "mom", split_axis=0, concat_axis=3, tiled=True),
        "energy",
        split_axis=1,
        concat_axis=3,
        tiled=True,
    )
    return result.reshape(green_ret.shape)


def solution(mesh):
    in_specs = (
        P("mom", "energy", None, None, None, None),
        P("mom", "energy", None, None, None, None),
        P(None, None, None, ("energy", "mom")),
        P(),
        P(),
    )
    out_specs = P("mom", "energy", None, None, None, None)
    return jax.shard_map(
        on_device, mesh=mesh, in_specs=in_specs, out_specs=out_specs, check_vma=False
    )
```

profile of v0, /device:TPU:1, one launch (start us, length us, event | category | flops | bytes accessed | tf_op | source)
XLA Modules:
  0.0 933.0 jit_solution(13167558090838878090)
XLA Ops:
  52.5 11.7 %fusion.85 = f32[1,10,128,128]{3,2,1,0:T(8,128)S(1)} fusion(f32[1,10,128,128]{3,2,1,0:T(8,128)S(1)} %fusion.97, f32[128,128]{1,0:T(8,128)S(1)} %fusion.88, f32[128,128]{1,0:T(8,128)S(1)} %fusion.196, f32[128,128]{1,0:T(8,128)S(1)} %fusion.86, f32[1,2,10,128,128]{4,3,1,2,0:T(8,128)S(1)} %get-tuple-element.47), kind=kOutput, calls=%fused_computation.183 | convolution fusion | flops 25198592 | bytes 327680 | tf_op jit(solution)/shard_map/eij,ekj->eik/dot_general | solution.py:40
  69.6 116.3 %copy.63 = f32[1,1,2,163840]{2,1,0,3:T(1,128)} copy(f32[1,1,2,163840]{3,0,2,1:T(1,128)S(1)} %bitcast.741) | data formatting | bytes 2621440 | tf_op jit(solution)/shard_map/reshape | solution.py:155
  186.6 230.7 %reduce = f32[163840,2]{1,0:T(8,128)} reduce(f32[163840,1,1,2]{3,2,1,0:T(1,128)} %bitcast.618, f32[]{:T(128)} %broadcast.330), dimensions={1,2}, to_apply=%bitcast.618.reduce_sub_computation | reduce | bytes 2621444
  417.3 60.7 %reshape.1577 = f32[32,1,10240]{2,1,0:T(1,128)S(1)} reshape(f32[163840,2]{1,0:T(8,128)} %reduce) | data formatting | bytes 2621440
  478.0 27.9 %all_to_all.69 = f32[32,1,10240]{2,1,0:T(1,128)S(1)} all-to-all(f32[32,1,10240]{2,1,0:T(1,128)S(1)} %reshape.1577), channel_id=1, replica_groups=mesh['energy'=32,'mom'=4] {'energy'}, dimensions={0} | all-to-all | bytes 2621440 | tf_op jit(solution)/shard_map/all_to_all | solution.py:159
  509.7 170.5 %reshape.1578 = f32[163840,1,1,2]{3,2,1,0:T(1,128)} reshape(f32[32,10240]{1,0:T(8,128)S(1)} %reduce.1) | data formatting | bytes 2621440
  680.2 43.3 %copy.79 = f32[1,1,2,32,5120]{4,3,2,1,0:T(8,128)S(1)} copy(f32[1,1,2,32,5120]{2,4,3,1,0:T(8,128)} %bitcast.77) | data formatting | bytes 2621440 | tf_op jit(solution)/shard_map/all_to_all | solution.py:159
  723.4 4.7 copy.65
  728.1 7.4 reshape.1579
  735.6 7.6 all-to-all-start.1
  745.7 15.2 %all-to-all-done.1 = f32[4,1,81920]{2,1,0:T(1,128)S(1)} async-done(((f32[4,1,81920]{2,1,0:T(1,128)}), f32[4,1,81920]{2,1,0:T(1,128)S(1)}, u32[]{:S(2)}, u32[]{:S(2)}) %all-to-all-start.1) | async-done | bytes 1310752 | tf_op jit(solution)/shard_map/all_to_all | solution.py:158
  760.9 5.5 reduce.2
  766.4 8.2 reshape.1580
  774.6 6.6 copy.80
  785.3 4.9 reshape.1440
  790.2 10.2 %fusion.231 = f32[128,20480]{1,0:T(8,128)S(1)} fusion(f32[32,20480]{1,0:T(8,128)} %reshape.1440, f32[64,32]{0,1:T(8,128)S(1)} %get-tuple-element.55, f32[64,32]{0,1:T(8,128)S(1)} %get-tuple-element.56), kind=kOutput, calls=%fused_computation.420 | convolution fusion | flops 1006637056 | bytes 13123584 | tf_op jit(solution)/shard_map/dot_general | solution.py:102
  805.0 7.8 squeeze.18
  812.7 11.7 %fusion.249 = (f32[64,8,1,1280]{3,2,1,0:T(1,128)}, f32[64,8,1,1280]{3,2,1,0:T(1,128)}) fusion(f32[64,8,2,1280]{3,2,1,0:T(2,128)} %squeeze.18), kind=kLoop, calls=%fused_computation.462 | loop fusion | bytes 10485760 | tf_op jit(solution)/shard_map/slice | solution.py:106
  824.5 7.8 squeeze.19
  832.3 11.7 %fusion.250 = (f32[64,8,1,1280]{3,2,1,0:T(1,128)}, f32[64,8,1,1280]{3,2,1,0:T(1,128)}) fusion(f32[64,8,2,1280]{3,2,1,0:T(2,128)} %squeeze.19), kind=kLoop, calls=%fused_computation.463 | loop fusion | bytes 10485760 | tf_op jit(solution)/shard_map/slice | solution.py:106
  869.1 5.7 fusion.15
  880.0 4.7 convolution_multiply_fusion
  885.9 21.1 %all_to_all.70 = f32[4,32,2,1280]{3,1,2,0:T(8,128)S(1)} all-to-all(f32[4,32,2,1280]{3,1,2,0:T(8,128)S(1)} %maximum_bitcast_fusion.2), channel_id=1, replica_groups=mesh['energy'=32,'mom'=4] {'mom'}, dimensions={0} | all-to-all | bytes 2621440 | tf_op jit(solution)/shard_map/all_to_all | solution.py:167
  909.0 21.9 %all_to_all.71 = f32[1,32,2,5120]{3,2,0,1:T(2,128)S(1)} all-to-all(f32[1,32,2,5120]{3,2,0,1:T(2,128)S(1)} %reshape.1576), channel_id=1, replica_groups=mesh['energy'=32,'mom'=4] {'energy'}, dimensions={1} | all-to-all | bytes 2621440 | tf_op jit(solution)/shard_map/all_to_all | solution.py:166
  (268 shorter events, 107.5 us)
Async XLA Ops:
  0.0 1.3 copy-start
  735.6 25.4 %all-to-all-start.1 = ((f32[4,1,81920]{2,1,0:T(1,128)}), f32[4,1,81920]{2,1,0:T(1,128)S(1)}, u32[]{:S(2)}, u32[]{:S(2)}) async-start(f32[4,1,81920]{2,1,0:T(1,128)} %reshape.1579), calls=%async_computation.1 | async-start | bytes 2621440 | tf_op jit(solution)/shard_map/all_to_all | solution.py:158
  743.2 2.2 copy-start.5
  848.0 1.5 copy-start.2
  857.1 1.5 copy-start.3
  867.4 1.7 copy-start.4
  930.9 1.7 copy-start.1
where the time goes:
time: 944 us; the launch traced here: 933 us
  local copies, waits for them, and re-layouts  502 us (53%)
  other arithmetic  259 us (27%)
  matrix products  76 us (8%)
  blocking collectives  70.9 us (8%)
  waiting for transfers between devices  15.2 us (2%)
    unnamed x18, local copies, waits for them, and re-layouts  253 us
    unnamed x1, other arithmetic  231 us
    reshape x1, local copies, waits for them, and re-layouts, on_device(): jnp.take(tiles_canon, canon_order, axis=2)  116 us
    all_to_all x2, local copies, waits for them, and re-layouts, on_device(): lax.all_to_all(lesser, 'energy', split_axis=3, concat_axis=1, tiled=True)  47.9 us
    all_to_all x1, blocking collectives, on_device(): lax.all_to_all(lesser, 'energy', split_axis=3, concat_axis=1, tiled=True)  27.9 us
    dot_general x52, matrix products, complex_mul(): ii = jnp.einsum(form, left[1], right[1], precision=lax.Precision.HIGHEST)  23.9 us
    slice x2, local copies, waits for them, and re-layouts, energy_mix(): spec_re = with_cos[:, :, 0] + with_sin[:, :, 1]  23.4 us
    all_to_all x1, blocking collectives, on_device(): lax.all_to_all(lax.all_to_all(mixed_pairs, 'mom', split_axis=0, concat_ax...  21.9 us
  transfers between devices with their start and end apart: 1, of which 1 were waited for; matrix products, arithmetic and copies ran while one was open for 0% of the time, Pallas kernels for 0%

commit v1 on v0

v1 whole, which is shorter than its diff:
```python
import functools
import math

import jax
import jax.numpy as jnp
import numpy as np
from jax import lax
from jax.experimental import pallas as pl
from jax.experimental.pallas import tpu as pltpu
from jax.sharding import PartitionSpec as P

MESH = pl.DeviceIdType.MESH
TILE = 128
NB = 4
KPTS = 4
NE = 32
NTILE = 10
ROWS = NTILE * TILE
NF = 2 * NE
NDEV = KPTS * NE
PER = ROWS // NDEV
CHUNKS = 2
STEP = PER // CHUNKS
F32 = jnp.float32
BF16 = jnp.bfloat16


def canon(i, j):
    if i == j:
        return i
    if j == i + 1:
        return NB + i
    return 2 * NB - 1 + j


def near(i):
    return [m for m in (i - 1, i, i + 1) if 0 <= m < NB]


TILES = [(i, i) for i in range(NB)] + [(i, i + 1) for i in range(NB - 1)] + [(i + 1, i) for i in range(NB - 1)]
CROSS = [(i, m) for i in range(NB) for m in range(NB) if abs(i - m) <= 2]


def split(x):
    high = x.astype(BF16)
    return high, (x - high.astype(F32)).astype(BF16)


def split_np(x):
    high = x.astype(jnp.bfloat16)
    low = (x - high.astype(np.float64)).astype(jnp.bfloat16)
    return high, low


def tables():
    phase = 2.0 * np.pi * (np.outer(np.arange(NF), np.arange(NE)) % NF) / NF
    cos, sin = np.cos(phase), np.sin(phase)
    forward = np.block([[cos, sin], [-sin, cos]])
    high, low = split_np(forward)
    forward3 = np.concatenate([high, high, low], axis=1)
    scale = 1.0 / math.sqrt(KPTS * NE) / NF
    cos, sin = cos.T * scale, sin.T * scale
    back = np.block([[-sin, -cos], [cos, -sin]])
    high, low = split_np(back)
    back3 = np.block([[high, high], [low, np.zeros_like(low)]])
    return forward3, back3


def dot(a, b):
    return lax.dot_general(a, b, (((1,), (0,)), ((), ())), preferred_element_type=F32)


def dot_t(a, b):
    return lax.dot_general(a, b, (((1,), (1,)), ((), ())), preferred_element_type=F32)


def peer(i, e, m):
    d = lax.rem(e * KPTS + m + i, NDEV)
    return d // KPTS, lax.rem(d, KPTS)


def kernel(tiles, mtab, fwd, bwd, green, scat, screened, out,
           gw, sw, cross, xs, lesc, send, recv, vin, vf, lf, back,
           in_sem, own_sem, a_send, a_recv, b_send, b_recv):
    e, m = lax.axis_index("energy"), lax.axis_index("mom")
    me = e * KPTS + m
    slot_me = m * NE + e

    barrier = pltpu.get_barrier_semaphore()

    @pl.loop(1, NDEV)
    def _(i):
        de, dm = peer(i, e, m)
        pl.semaphore_signal(barrier, inc=1, device_id=(de, dm), device_id_type=MESH)

    loads = []
    for q in range(KPTS):
        for c in range(2):
            loads.append(pltpu.make_async_copy(screened.at[q, :, c, :], vin.at[q, c], in_sem.at[q * 2 + c]))
            loads[-1].start()

    order = []
    for t in range(NTILE):
        row, col = tiles[t, 0], tiles[t, 1]
        off = col - row
        order.append(jnp.where(off == 0, row, jnp.where(off == 1, NB + row, 2 * NB - 1 + col)))
    slot = []
    for p in range(NTILE):
        total = jnp.int32(0)
        for t in range(NTILE):
            total = jnp.where(order[t] == p, t, total)
        slot.append(total)

    for p in range(NTILE):
        s = slot[p]
        for src, dst, flip in ((green, gw, False), (scat, sw, True)):
            re, im = split(src[0, s]), split(src[1, s])
            for h in range(2):
                dst[p, h, 0:TILE, 0:TILE] = re[h]
                dst[p, h, 0:TILE, TILE:] = im[h]
                dst[p, h, TILE:, 0:TILE] = -im[h]
                dst[p, h, TILE:, TILE:] = re[h]

    started = set()
    for k, mm in TILES:
        rows = near(k)
        w = canon(k, mm)
        high = [gw[canon(i, k), 0, 0:TILE, :] for i in rows]
        low = [gw[canon(i, k), 1, 0:TILE, :] for i in rows]
        n = len(rows) * TILE
        r1 = dot(jnp.concatenate(high + low, axis=0), sw[w, 0])
        r2 = dot(jnp.concatenate(high, axis=0), sw[w, 1])
        total = r1[:n] + (r1[n:] + r2)
        for a, i in enumerate(rows):
            x = CROSS.index((i, mm))
            part = total[a * TILE:(a + 1) * TILE]
            if x in started:
                cross[x] = cross[x] + part
            else:
                cross[x] = part
                started.add(x)
    for x in range(len(CROSS)):
        high, low = split(cross[x])
        xs[x, 0] = high
        xs[x, 1] = low
    started = set()
    for j, mm in TILES:
        rows = near(j)
        w = canon(j, mm)
        high = [xs[CROSS.index((i, mm)), 0] for i in rows]
        low = [xs[CROSS.index((i, mm)), 1] for i in rows]
        n = len(rows) * TILE
        r1 = dot_t(jnp.concatenate(high + low, axis=0), gw[w, 0])
        r2 = dot_t(jnp.concatenate(high, axis=0), gw[w, 1])
        total = r1[:n] + (r1[n:] + r2)
        for a, i in enumerate(rows):
            p = canon(i, j)
            part = total[a * TILE:(a + 1) * TILE]
            if p in started:
                lesc[p] = lesc[p] + part
            else:
                lesc[p] = part
                started.add(p)
    for t in range(NTILE):
        tile = lesc[order[t]]
        send[0, t * TILE:(t + 1) * TILE, :] = tile[:, 0:TILE]
        send[1, t * TILE:(t + 1) * TILE, :] = tile[:, TILE:]

    pl.semaphore_wait(barrier, NDEV - 1)

    def part(ref, index, h):
        return ref.at[:, pl.ds(index * PER + h * STEP, STEP), :]

    def total_of(ref):
        return ref.at[:, pl.ds(0, (NDEV - 1) * STEP), :]

    own = []
    for h in range(CHUNKS):
        @pl.loop(1, NDEV)
        def _(i):
            de, dm = peer(i, e, m)
            pltpu.make_async_remote_copy(
                part(send, de * KPTS + dm, h), part(recv, slot_me, h), a_send.at[h], a_recv.at[h],
                device_id=(de, dm), device_id_type=MESH).start()

        own.append(pltpu.make_async_copy(part(send, me, h), part(recv, slot_me, h), own_sem.at[h]))
        own[-1].start()

    for copy in loads:
        copy.wait()

    def transform(pieces, dst, j, count):
        high, low = [], []
        for piece in pieces:
            a, b = split(piece)
            high.append(a)
            low.append(b)
        high, low = jnp.concatenate(high, axis=1), jnp.concatenate(low, axis=1)
        freq = dot(fwd[...], jnp.concatenate([high, low, high], axis=0))
        for k in range(count):
            dst[k, j] = freq[:, k * TILE:(k + 1) * TILE]

    for j in range(PER):
        lanes = slice(j * TILE, (j + 1) * TILE)
        transform([vin[q, :, :, lanes].reshape(2 * NE, TILE) for q in range(KPTS)], vf, j, KPTS)

    a_done = []
    b_done = []
    for h in range(CHUNKS):
        own[h].wait()
        pltpu.make_async_remote_copy(
            total_of(send), total_of(recv), a_send.at[h], a_recv.at[h], device_id=(e, m), device_id_type=MESH).wait_recv()
        for j in range(h * STEP, (h + 1) * STEP):
            pieces = []
            for k in range(KPTS):
                both = [recv[c, pl.ds(k * NE * PER + j, NE, stride=PER), :] for c in range(2)]
                pieces.append(jnp.concatenate(both, axis=0))
            transform(pieces, lf, j, KPTS)
            high, low = [], []
            for k in range(KPTS):
                sum_re = sum_im = None
                for q in range(KPTS):
                    left = lf[mtab[k, q], j]
                    right = vf[q, j]
                    lr, li, vr, vi = left[:NF], left[NF:], right[:NF], right[NF:]
                    re, im = lr * vr - li * vi, lr * vi + li * vr
                    sum_re = re if sum_re is None else sum_re + re
                    sum_im = im if sum_im is None else sum_im + im
                a, b = split(jnp.concatenate([sum_re, sum_im], axis=0))
                high.append(a)
                low.append(b)
            stacked = jnp.concatenate([jnp.concatenate(high, axis=1), jnp.concatenate(low, axis=1)], axis=0)
            res = dot(bwd[...], stacked)
            res = res[:2 * NE] + res[2 * NE:]
            for k in range(KPTS):
                for c in range(2):
                    back[c, pl.ds(k * NE * PER + j, NE, stride=PER), :] = res[c * NE:(c + 1) * NE, k * TILE:(k + 1) * TILE]

        @pl.loop(1, NDEV)
        def _(i):
            de, dm = peer(i, e, m)
            pltpu.make_async_remote_copy(
                part(back, dm * NE + de, h), part(out, me, h), b_send.at[h], b_recv.at[h],
                device_id=(de, dm), device_id_type=MESH).start()

        last = pltpu.make_async_copy(part(back, slot_me, h), part(out, me, h), own_sem.at[CHUNKS + h])
        last.start()
        b_done.append(last)

    for h in range(CHUNKS):
        b_done[h].wait()
        pltpu.make_async_remote_copy(
            total_of(send), total_of(recv), a_send.at[h], a_recv.at[h], device_id=(e, m), device_id_type=MESH).wait_send()
        pltpu.make_async_remote_copy(
            total_of(back), total_of(out), b_send.at[h], b_recv.at[h], device_id=(e, m), device_id_type=MESH).wait()


def on_device(green_ret, scatter_in, screened, momentum_table, tile_list, fwd, bwd):
    green = green_ret.reshape(2, NTILE, TILE, TILE)
    scat = scatter_in.reshape(2, NTILE, TILE, TILE)
    vmem = pl.BlockSpec(memory_space=pltpu.VMEM)
    smem = pl.BlockSpec(memory_space=pltpu.SMEM)
    hbm = pl.BlockSpec(memory_space=pl.ANY)
    dma = pltpu.SemaphoreType.DMA
    out = pl.pallas_call(
        kernel,
        out_shape=jax.ShapeDtypeStruct((2, ROWS, TILE), F32),
        in_specs=[smem, smem, vmem, vmem, vmem, vmem, hbm],
        out_specs=hbm,
        scratch_shapes=[
            pltpu.VMEM((NTILE, 2, 2 * TILE, 2 * TILE), BF16),
            pltpu.VMEM((NTILE, 2, 2 * TILE, 2 * TILE), BF16),
            pltpu.VMEM((len(CROSS), TILE, 2 * TILE), F32),
            pltpu.VMEM((len(CROSS), 2, TILE, 2 * TILE), BF16),
            pltpu.VMEM((NTILE, TILE, 2 * TILE), F32),
            pltpu.VMEM((2, ROWS, TILE), F32),
            pltpu.VMEM((2, ROWS, TILE), F32),
            pltpu.VMEM((KPTS, 2, NE, ROWS), F32),
            pltpu.VMEM((KPTS, PER, 2 * NF, TILE), F32),
            pltpu.VMEM((KPTS, PER, 2 * NF, TILE), F32),
            pltpu.VMEM((2, ROWS, TILE), F32),
            dma((2 * KPTS,)),
            dma((2 * CHUNKS,)),
            dma((CHUNKS,)),
            dma((CHUNKS,)),
            dma((CHUNKS,)),
            dma((CHUNKS,)),
        ],
        compiler_params=pltpu.CompilerParams(
            collective_id=0, has_side_effects=True, vmem_limit_bytes=60 * 1024 * 1024
        ),
        name="born_exchange",
    )(tile_list, momentum_table, fwd, bwd, green, scat, screened)
    return out.reshape(green_ret.shape)


def solution(mesh):
    forward, backward = tables()
    in_specs = (
        P("mom", "energy", None, None, None, None),
        P("mom", "energy", None, None, None, None),
        P(None, None, None, ("energy", "mom")),
        P(),
        P(),
        P(),
        P(),
    )
    out_specs = P("mom", "energy", None, None, None, None)
    step = jax.shard_map(
        on_device, mesh=mesh, in_specs=in_specs, out_specs=out_specs, check_vma=False
    )

    def run(green_ret, scatter_in, screened, momentum_table, tile_list):
        return step(
            green_ret, scatter_in, screened, momentum_table, tile_list,
            jnp.asarray(forward), jnp.asarray(backward),
        )

    return run
```

time: 944 us -> 52.6 us (0.06); the launches traced: 933 us -> 52.4 us
  local copies, waits for them, and re-layouts: 502 us -> 3.86 us
  other arithmetic: 259 us -> 0 us
  matrix products: 76 us -> 0 us
  blocking collectives: 70.9 us -> 0 us
  Pallas kernels: 0 us -> 48.6 us
  waiting for transfers between devices: 15.2 us -> 0 us
    unnamed x18 -> x2, local copies, waits for them, and re-layouts: 253 us -> 3.86 us
    unnamed x1 -> x0, other arithmetic: 231 us -> none
    reshape x3 -> x0, local copies, waits for them, and re-layouts: 122 us -> none  [the longest x1 116 us: on_device(): jnp.take(tiles_canon, canon_order, axis=2)]
    dot_general x210 -> x0, matrix products: 76 us -> none  [the longest x52 23.9 us: complex_mul(): ii = jnp.einsum(form, left[1], right[1], precision=lax.Precision.HIGHEST)]
    all_to_all x3 -> x0, blocking collectives: 70.9 us -> none  [the longest x1 27.9 us: on_device(): lax.all_to_all(lesser, 'energy', split_axis=3, concat_axis=1, tiled=True)]
    all_to_all x6 -> x0, local copies, waits for them, and re-layouts: 56.9 us -> none  [the longest x2 47.9 us: on_device(): lax.all_to_all(lesser, 'energy', split_axis=3, concat_axis=1, tiled=True)]
    pallas_call x0 -> x1, Pallas kernels: none -> 48.6 us  [on_device(): pl.pallas_call(kernel, out_shape=jax.ShapeDtypeStruct((2, ROWS, TILE), F3...]
    slice x5 -> x0, local copies, waits for them, and re-layouts: 28.2 us -> none  [the longest x2 23.4 us: energy_mix(): spec_re = with_cos[:, :, 0] + with_sin[:, :, 1]]
  transfers between devices with their start and end apart: 1 -> 0, of which waited for: 1 -> 0; matrix products, arithmetic and copies ran while one was open for 0% -> 0% of each run, Pallas kernels for 0% -> 0%
where the time goes in v1:
time: 52.6 us; the launch traced here: 52.4 us
  Pallas kernels  48.6 us (92%)
  local copies, waits for them, and re-layouts  3.86 us (7%)
    pallas_call x1, Pallas kernels, on_device(): pl.pallas_call(kernel, out_shape=jax.ShapeDtypeStruct((2, ROWS, TILE), F3...  48.6 us
    unnamed x2, local copies, waits for them, and re-layouts  3.86 us

profile of v1, /device:TPU:1, one launch (start us, length us, event | category | flops | bytes accessed | tf_op | source)
XLA Modules:
  0.0 52.4 jit_solution(5341926012174546642)
XLA Ops:
  0.0 1.4 %copy.8.tiles = s32[10,2]{1,0:T(8,128)} copy(s32[10,2]{0,1:T(2,128)} %param.11) | data formatting | bytes 160 | tf_op args[4]
  1.4 48.6 %born_exchange.1 = f32[2,1280,128]{2,1,0:T(8,128)} custom-call(s32[10,2]{1,0:T(8,128)} %copy.8.tiles, s32[4,4]{1,0:T(4,128)} %mtab.1, bf16[128,192]{1,0:T(8,128)(2,1)} %constant.4.clone.fwd, bf16[128,256]{1,0:T(8,128)(2,1)} %constant.5.clone.bwd, f32[2,10,128,128]{3,2,1,0:T(8,128)} %bitcast.4, f32[2,10,128,128]{3,2,1,0:T(8,128)} %bitcast.5, ...), custom_call_target="tpu_custom_call" | custom-call | tf_op jit(solution)/shard_map/born_exchange/pallas_call | solution.py:265
  49.9 2.5 %copy.10 = f32[1,1,2,10,128,128]{5,4,3,2,1,0:T(8,128)} copy(f32[1,1,2,10,128,128]{5,4,3,2,1,0:T(8,128)} %bitcast.3) | data formatting | bytes 2621440

commit v2 on v1

--- a/solution.py
+++ b/solution.py
@@ -9,7 +9,7 @@
 from jax.experimental.pallas import tpu as pltpu
 from jax.sharding import PartitionSpec as P
 
-MESH = pl.DeviceIdType.MESH
+FLAT = pl.DeviceIdType.LOGICAL
 TILE = 128
 NB = 4
 KPTS = 4
@@ -74,24 +74,25 @@
     return lax.dot_general(a, b, (((1,), (1,)), ((), ())), preferred_element_type=F32)
 
 
-def peer(i, e, m):
-    d = lax.rem(e * KPTS + m + i, NDEV)
-    return d // KPTS, lax.rem(d, KPTS)
-
-
-def kernel(tiles, mtab, fwd, bwd, green, scat, screened, out,
-           gw, sw, cross, xs, lesc, send, recv, vin, vf, lf, back,
-           in_sem, own_sem, a_send, a_recv, b_send, b_recv):
+def peer(i, me):
+    return (me + i * 27) & (NDEV - 1)
+
+
+def kernel(tiles, mtab, fwd, bwd, green_in, scat_in, screened, out,
+           green, scat, gw, sw, cross, xs, lesc, send, recv, vin, vf, lf, back,
+           tile_sem, in_sem, own_sem, a_send, a_recv, b_send, b_recv):
     e, m = lax.axis_index("energy"), lax.axis_index("mom")
     me = e * KPTS + m
     slot_me = m * NE + e
 
+    first = [pltpu.make_async_copy(green_in, green, tile_sem.at[0]), pltpu.make_async_copy(scat_in, scat, tile_sem.at[1])]
+    for copy in first:
+        copy.start()
     barrier = pltpu.get_barrier_semaphore()
 
     @pl.loop(1, NDEV)
     def _(i):
-        de, dm = peer(i, e, m)
-        pl.semaphore_signal(barrier, inc=1, device_id=(de, dm), device_id_type=MESH)
+        pl.semaphore_signal(barrier, inc=1, device_id=peer(i, me), device_id_type=FLAT)
 
     loads = []
     for q in range(KPTS):
@@ -101,7 +102,7 @@
 
     order = []
     for t in range(NTILE):
-        row, col = tiles[t, 0], tiles[t, 1]
+        row, col = tiles[0, t], tiles[1, t]
         off = col - row
         order.append(jnp.where(off == 0, row, jnp.where(off == 1, NB + row, 2 * NB - 1 + col)))
     slot = []
@@ -111,6 +112,8 @@
             total = jnp.where(order[t] == p, t, total)
         slot.append(total)
 
+    for copy in first:
+        copy.wait()
     for p in range(NTILE):
         s = slot[p]
         for src, dst, flip in ((green, gw, False), (scat, sw, True)):
@@ -178,10 +181,10 @@
     for h in range(CHUNKS):
         @pl.loop(1, NDEV)
         def _(i):
-            de, dm = peer(i, e, m)
+            d = peer(i, me)
             pltpu.make_async_remote_copy(
-                part(send, de * KPTS + dm, h), part(recv, slot_me, h), a_send.at[h], a_recv.at[h],
-                device_id=(de, dm), device_id_type=MESH).start()
+                part(send, d, h), part(recv, slot_me, h), a_send.at[h], a_recv.at[h],
+                device_id=d, device_id_type=FLAT).start()
 
         own.append(pltpu.make_async_copy(part(send, me, h), part(recv, slot_me, h), own_sem.at[h]))
         own[-1].start()
@@ -209,7 +212,7 @@
     for h in range(CHUNKS):
         own[h].wait()
         pltpu.make_async_remote_copy(
-            total_of(send), total_of(recv), a_send.at[h], a_recv.at[h], device_id=(e, m), device_id_type=MESH).wait_recv()
+            total_of(send), total_of(recv), a_send.at[h], a_recv.at[h], device_id=me, device_id_type=FLAT).wait_recv()
         for j in range(h * STEP, (h + 1) * STEP):
             pieces = []
             for k in range(KPTS):
@@ -238,10 +241,10 @@
 
         @pl.loop(1, NDEV)
         def _(i):
-            de, dm = peer(i, e, m)
+            d = peer(i, me)
             pltpu.make_async_remote_copy(
-                part(back, dm * NE + de, h), part(out, me, h), b_send.at[h], b_recv.at[h],
-                device_id=(de, dm), device_id_type=MESH).start()
+                part(back, (d & (KPTS - 1)) * NE + (d >> 2), h), part(out, me, h), b_send.at[h], b_recv.at[h],
+                device_id=d, device_id_type=FLAT).start()
 
         last = pltpu.make_async_copy(part(back, slot_me, h), part(out, me, h), own_sem.at[CHUNKS + h])
         last.start()
@@ -250,9 +253,9 @@
     for h in range(CHUNKS):
         b_done[h].wait()
         pltpu.make_async_remote_copy(
-            total_of(send), total_of(recv), a_send.at[h], a_recv.at[h], device_id=(e, m), device_id_type=MESH).wait_send()
+            total_of(send), total_of(recv), a_send.at[h], a_recv.at[h], device_id=me, device_id_type=FLAT).wait_send()
         pltpu.make_async_remote_copy(
-            total_of(back), total_of(out), b_send.at[h], b_recv.at[h], device_id=(e, m), device_id_type=MESH).wait()
+            total_of(back), total_of(out), b_send.at[h], b_recv.at[h], device_id=me, device_id_type=FLAT).wait()
 
 
 def on_device(green_ret, scatter_in, screened, momentum_table, tile_list, fwd, bwd):
@@ -264,10 +267,12 @@
     dma = pltpu.SemaphoreType.DMA
     out = pl.pallas_call(
         kernel,
-        out_shape=jax.ShapeDtypeStruct((2, ROWS, TILE), F32),
-        in_specs=[smem, smem, vmem, vmem, vmem, vmem, hbm],
-        out_specs=hbm,
+        out_shape=pltpu.VMEM((2, ROWS, TILE), F32),
+        in_specs=[smem, smem, vmem, vmem, hbm, hbm, hbm],
+        out_specs=vmem,
         scratch_shapes=[
+            pltpu.VMEM((2, NTILE, TILE, TILE), F32),
+            pltpu.VMEM((2, NTILE, TILE, TILE), F32),
             pltpu.VMEM((NTILE, 2, 2 * TILE, 2 * TILE), BF16),
             pltpu.VMEM((NTILE, 2, 2 * TILE, 2 * TILE), BF16),
             pltpu.VMEM((len(CROSS), TILE, 2 * TILE), F32),
@@ -279,6 +284,7 @@
             pltpu.VMEM((KPTS, PER, 2 * NF, TILE), F32),
             pltpu.VMEM((KPTS, PER, 2 * NF, TILE), F32),
             pltpu.VMEM((2, ROWS, TILE), F32),
+            dma((2,)),
             dma((2 * KPTS,)),
             dma((2 * CHUNKS,)),
             dma((CHUNKS,)),
@@ -290,7 +296,7 @@
             collective_id=0, has_side_effects=True, vmem_limit_bytes=60 * 1024 * 1024
         ),
         name="born_exchange",
-    )(tile_list, momentum_table, fwd, bwd, green, scat, screened)
+    )(tile_list.T, momentum_table, fwd, bwd, green, scat, screened)
     return out.reshape(green_ret.shape)
 
 

time: 52.6 us -> 45.7 us (0.87)
  Pallas kernels: 48.6 us -> 44.5 us
  local copies, waits for them, and re-layouts: 3.86 us -> 1.06 us
    pallas_call x1, Pallas kernels: 48.6 us -> 44.5 us  [on_device(): pl.pallas_call(kernel, out_shape=pltpu.VMEM((2, ROWS, TILE), F32), in_spe...]
    unnamed x2 -> x1, local copies, waits for them, and re-layouts: 3.86 us -> 1.06 us
where the time goes in v2:
time: 45.7 us; the launch traced here: 45.5 us
  Pallas kernels  44.5 us (97%)
  local copies, waits for them, and re-layouts  1.06 us (2%)
    pallas_call x1, Pallas kernels, on_device(): pl.pallas_call(kernel, out_shape=pltpu.VMEM((2, ROWS, TILE), F32), in_spe...  44.5 us
    unnamed x1, local copies, waits for them, and re-layouts  1.06 us

profile of v2, /device:TPU:1, one launch (start us, length us, event | category | flops | bytes accessed | tf_op | source)
XLA Modules:
  0.0 45.5 jit_solution(9705813224709272234)
XLA Ops:
  0.0 44.5 %born_exchange.1 = f32[2,1280,128]{2,1,0:T(8,128)S(1)} custom-call(s32[2,10]{1,0:T(2,128)} %bitcast.7, s32[4,4]{1,0:T(4,128)} %mtab.1, bf16[128,192]{1,0:T(8,128)(2,1)} %constant.4.clone.fwd, bf16[128,256]{1,0:T(8,128)(2,1)} %constant.5.clone.bwd, f32[2,10,128,128]{3,2,1,0:T(8,128)} %bitcast.5, f32[2,10,128,128]{3,2,1,0:T(8,128)} %bitcast.6, ...), custom_call_target="tpu_custom_call" | custom-call | tf_op jit(solution)/shard_map/born_exchange/pallas_call | solution.py:268
  44.5 1.1 %copy.9 = f32[1,1,2,10,128,128]{5,4,3,2,1,0:T(8,128)} copy(f32[1,1,2,10,128,128]{5,4,3,2,1,0:T(8,128)S(1)} %bitcast.4) | data formatting | bytes 2621440

commit v3 on v2

--- a/solution.py
+++ b/solution.py
@@ -219,6 +219,7 @@
                 both = [recv[c, pl.ds(k * NE * PER + j, NE, stride=PER), :] for c in range(2)]
                 pieces.append(jnp.concatenate(both, axis=0))
             transform(pieces, lf, j, KPTS)
+        for j in range(h * STEP, (h + 1) * STEP):
             high, low = [], []
             for k in range(KPTS):
                 sum_re = sum_im = None

time: 45.7 us -> 45.4 us (level)
  no operation moved by 1% of the time
where the time goes in v3:
time: 45.4 us; the launch traced here: 45.2 us
  Pallas kernels  44.2 us (97%)
  local copies, waits for them, and re-layouts  1.06 us (2%)
    pallas_call x1, Pallas kernels, on_device(): pl.pallas_call(kernel, out_shape=pltpu.VMEM((2, ROWS, TILE), F32), in_spe...  44.2 us
    unnamed x1, local copies, waits for them, and re-layouts  1.06 us

profile of v3, /device:TPU:1, one launch (start us, length us, event | category | flops | bytes accessed | tf_op | source)
XLA Modules:
  0.0 45.2 jit_solution(8310281399818962664)
XLA Ops:
  0.0 44.2 %born_exchange.1 = f32[2,1280,128]{2,1,0:T(8,128)S(1)} custom-call(s32[2,10]{1,0:T(2,128)} %bitcast.7, s32[4,4]{1,0:T(4,128)} %mtab.1, bf16[128,192]{1,0:T(8,128)(2,1)} %constant.4.clone.fwd, bf16[128,256]{1,0:T(8,128)(2,1)} %constant.5.clone.bwd, f32[2,10,128,128]{3,2,1,0:T(8,128)} %bitcast.5, f32[2,10,128,128]{3,2,1,0:T(8,128)} %bitcast.6, ...), custom_call_target="tpu_custom_call" | custom-call | tf_op jit(solution)/shard_map/born_exchange/pallas_call | solution.py:269
  44.2 1.1 %copy.9 = f32[1,1,2,10,128,128]{5,4,3,2,1,0:T(8,128)} copy(f32[1,1,2,10,128,128]{5,4,3,2,1,0:T(8,128)S(1)} %bitcast.4) | data formatting | bytes 2621440

commit v4 on v3

--- a/solution.py
+++ b/solution.py
@@ -74,8 +74,8 @@
     return lax.dot_general(a, b, (((1,), (1,)), ((), ())), preferred_element_type=F32)
 
 
-def peer(i, me):
-    return (me + i * 27) & (NDEV - 1)
+def peer(i, me, stride=27):
+    return (me + i * stride) & (NDEV - 1)
 
 
 def kernel(tiles, mtab, fwd, bwd, green_in, scat_in, screened, out,
@@ -90,8 +90,7 @@
         copy.start()
     barrier = pltpu.get_barrier_semaphore()
 
-    @pl.loop(1, NDEV)
-    def _(i):
+    for i in range(1, NDEV):
         pl.semaphore_signal(barrier, inc=1, device_id=peer(i, me), device_id_type=FLAT)
 
     loads = []
@@ -242,7 +241,7 @@
 
         @pl.loop(1, NDEV)
         def _(i):
-            d = peer(i, me)
+            d = peer(i, me, 59)
             pltpu.make_async_remote_copy(
                 part(back, (d & (KPTS - 1)) * NE + (d >> 2), h), part(out, me, h), b_send.at[h], b_recv.at[h],
                 device_id=d, device_id_type=FLAT).start()

time: 45.4 us -> 45 us (level)
  no operation moved by 1% of the time
where the time goes in v4:
time: 45 us; the launch traced here: 44.8 us
  Pallas kernels  43.8 us (97%)
  local copies, waits for them, and re-layouts  1.06 us (2%)
    pallas_call x1, Pallas kernels, on_device(): pl.pallas_call(kernel, out_shape=pltpu.VMEM((2, ROWS, TILE), F32), in_spe...  43.8 us
    unnamed x1, local copies, waits for them, and re-layouts  1.06 us

profile of v4, /device:TPU:1, one launch (start us, length us, event | category | flops | bytes accessed | tf_op | source)
XLA Modules:
  0.0 44.8 jit_solution(17907927107122370844)
XLA Ops:
  0.0 43.8 %born_exchange.1 = f32[2,1280,128]{2,1,0:T(8,128)S(1)} custom-call(s32[2,10]{1,0:T(2,128)} %bitcast.7, s32[4,4]{1,0:T(4,128)} %mtab.1, bf16[128,192]{1,0:T(8,128)(2,1)} %constant.4.clone.fwd, bf16[128,256]{1,0:T(8,128)(2,1)} %constant.5.clone.bwd, f32[2,10,128,128]{3,2,1,0:T(8,128)} %bitcast.5, f32[2,10,128,128]{3,2,1,0:T(8,128)} %bitcast.6, ...), custom_call_target="tpu_custom_call" | custom-call | tf_op jit(solution)/shard_map/born_exchange/pallas_call | solution.py:268
  43.8 1.1 %copy.9 = f32[1,1,2,10,128,128]{5,4,3,2,1,0:T(8,128)} copy(f32[1,1,2,10,128,128]{5,4,3,2,1,0:T(8,128)S(1)} %bitcast.4) | data formatting | bytes 2621440
